TPU v7x, 128 devices: a whole 4x4x4 slice. The times are simulated.
128 devices in a mesh: cam: 4 (over z_hi, core), lmk: 32 (over y, z_lo, x).
Axes of the slice: x: 4, y: 4, z: 4 (z_hi: 2, z_lo: 2; z = z_hi * 2 + z_lo), core: 2. Of those that a mesh axis runs over, the one named last changes fastest.
Arguments:
- probes: bfloat16 [128, 32, 576], P(('cam', 'lmk')), may hold values from -6 to 6
- u_inverse: bfloat16 [128, 576, 576], P(('cam', 'lmk')), may hold values from -1 to 3
- couplings: bfloat16 [10240, 576, 192], P(('cam', 'lmk')), may hold values from -0.09375 to 0.09375
- v_inverse: bfloat16 [1536, 192, 192], P('lmk'), may hold values from -3 to 4
- tile_cam: int32 [10240], P(('cam', 'lmk')), may hold values from 0 to 31
- tile_lmk: int32 [10240], P(('cam', 'lmk')), may hold values from 0 to 47
Outputs:
- solution: float32 [128, 32, 576], P(('cam', 'lmk'))
All inputs are finite; a program needn't handle non-finite values.
Results may differ from a plain program's by a relative error of at most 0.012.
Values may be sent and summed in bfloat16 or wider, within the bound.
A program may use at most 128 MiB of HBM per device.

v0:
```python
import functools

import jax
import jax.numpy as jnp
from jax import lax
from jax.experimental import pallas as pl
from jax.experimental.pallas import tpu as pltpu
from jax.sharding import PartitionSpec as P

POWERS = 4
MESH = pl.DeviceIdType.MESH
AXES = ("cam", "lmk")
COLLECTIVE_IDS = {}


def exchange_kernel(n, axis, gather, x_ref, o_ref, send_sem, recv_sem, local_sem):
    me = lax.axis_index(axis)
    coords = tuple(lax.axis_index(name) for name in AXES)
    slot = AXES.index(axis)

    def device(peer):
        return coords[:slot] + (peer,) + coords[slot + 1:]

    barrier = pltpu.get_barrier_semaphore()
    for step in range(1, n):
        pl.semaphore_signal(barrier, inc=1, device_id=device(lax.rem(me + step, n)), device_id_type=MESH)
    pl.semaphore_wait(barrier, n - 1)
    local = pltpu.make_async_copy(x_ref if gather else x_ref.at[me], o_ref.at[me], local_sem)
    local.start()
    sends = []
    for step in range(1, n):
        peer = lax.rem(me + step, n)
        copy = pltpu.make_async_remote_copy(
            src_ref=x_ref if gather else x_ref.at[peer],
            dst_ref=o_ref.at[me],
            send_sem=send_sem.at[step],
            recv_sem=recv_sem.at[step],
            device_id=device(peer),
            device_id_type=MESH,
        )
        copy.start()
        sends.append(copy)
    local.wait()
    for copy in sends:
        copy.wait_send()
    for step in range(1, n):
        source = lax.rem(me + n - step, n)
        pltpu.make_async_remote_copy(
            src_ref=o_ref.at[source],
            dst_ref=o_ref.at[source],
            send_sem=send_sem.at[step],
            recv_sem=recv_sem.at[step],
            device_id=device(source),
            device_id_type=MESH,
        ).wait_recv()


def exchange(x, axis_name, gather=False):
    n = lax.axis_size(axis_name)
    key = (axis_name, gather, x.shape, str(x.dtype))
    if key not in COLLECTIVE_IDS:
        COLLECTIVE_IDS[key] = len(COLLECTIVE_IDS)
    shape = (n,) + x.shape if gather else x.shape
    return pl.pallas_call(
        functools.partial(exchange_kernel, n, axis_name, gather),
        out_shape=jax.ShapeDtypeStruct(shape, x.dtype),
        in_specs=[pl.BlockSpec(memory_space=pl.ANY)],
        out_specs=pl.BlockSpec(memory_space=pl.ANY),
        scratch_shapes=[
            pltpu.SemaphoreType.DMA((n,)),
            pltpu.SemaphoreType.DMA((n,)),
            pltpu.SemaphoreType.DMA,
        ],
        compiler_params=pltpu.CompilerParams(collective_id=COLLECTIVE_IDS[key], has_side_effects=True),
    )(x)


def onehot_sum(selected, values):
    upper = values.astype(jnp.bfloat16)
    lower = (values - upper.astype(jnp.float32)).astype(jnp.bfloat16)
    first = jnp.einsum("st,tpx->spx", selected, upper, preferred_element_type=jnp.float32)
    second = jnp.einsum("st,tpx->spx", selected, lower, preferred_element_type=jnp.float32)
    return first + second


def a2a_gather(block, axis_name):
    size = lax.axis_size(axis_name)
    if axis_name == "cam":
        got = exchange(block, axis_name, gather=True)
    else:
        tiled = jnp.broadcast_to(block[None], (size,) + block.shape)
        got = lax.all_to_all(tiled, axis_name, 0, 0, tiled=False)
    return got.reshape((size * block.shape[0],) + block.shape[1:])


def a2a_reduce_scatter(full, axis_name):
    size = lax.axis_size(axis_name)
    chunks = full.reshape((size, full.shape[0] // size) + full.shape[1:])
    if axis_name == "cam":
        got = exchange(chunks.astype(jnp.bfloat16), axis_name)
    else:
        got = lax.all_to_all(chunks.astype(jnp.bfloat16), axis_name, 0, 0, tiled=False)
    return jnp.sum(got.astype(jnp.float32), axis=0)


def swap_kernel(x_ref, o_ref, send_sem, recv_sem, *, partner):
    barrier = pltpu.get_barrier_semaphore()
    pl.semaphore_signal(barrier, inc=1, device_id=partner(), device_id_type=MESH)
    pl.semaphore_wait(barrier, 1)
    copy = pltpu.make_async_remote_copy(
        src_ref=x_ref,
        dst_ref=o_ref,
        send_sem=send_sem,
        recv_sem=recv_sem,
        device_id=partner(),
        device_id_type=MESH,
    )
    copy.start()
    copy.wait_send()
    copy.wait_recv()


def swap(x, flip):
    key = ("swap", flip, x.shape, str(x.dtype))
    if key not in COLLECTIVE_IDS:
        COLLECTIVE_IDS[key] = len(COLLECTIVE_IDS)

    def partner():
        return (lax.axis_index("cam") ^ flip, lax.axis_index("lmk"))

    return pl.pallas_call(
        functools.partial(swap_kernel, partner=partner),
        out_shape=jax.ShapeDtypeStruct(x.shape, x.dtype),
        in_specs=[pl.BlockSpec(memory_space=pl.ANY)],
        out_specs=pl.BlockSpec(memory_space=pl.ANY),
        scratch_shapes=[pltpu.SemaphoreType.DMA, pltpu.SemaphoreType.DMA],
        compiler_params=pltpu.CompilerParams(collective_id=COLLECTIVE_IDS[key], has_side_effects=True),
    )(x)


def pick(flag, a, b):
    return jnp.where(flag == 0, a, b)


def cam_reduce(partial_value):
    cam = lax.axis_index("cam")
    core, high = cam % 2, cam // 2
    chunks = partial_value.reshape((2, 2, partial_value.shape[0] // 4) + partial_value.shape[1:])
    mine = pick(core, chunks[:, 0], chunks[:, 1])
    theirs = pick(core, chunks[:, 1], chunks[:, 0])
    chip = mine + swap(theirs.astype(jnp.bfloat16), 1).astype(jnp.float32)
    keep = pick(high, chip[0], chip[1])
    send = pick(high, chip[1], chip[0])
    return keep + swap(send.astype(jnp.bfloat16), 2).astype(jnp.float32)


def cam_gather(block):
    cam = lax.axis_index("cam")
    core, high = cam % 2, cam // 2
    other = swap(block, 2)
    pair = pick(high, jnp.stack([block, other]), jnp.stack([other, block]))
    other_pair = swap(pair, 1)
    full = pick(core, jnp.stack([pair, other_pair], axis=1), jnp.stack([other_pair, pair], axis=1))
    return full.reshape((4 * block.shape[0],) + block.shape[1:])


def local(probes, u_inverse, couplings, v_inverse, tile_cam, tile_lmk):
    group_size = lax.axis_size("lmk") * u_inverse.shape[0]
    landmark_count = v_inverse.shape[0]
    cam_onehot = (tile_cam[None, :] == jnp.arange(group_size, dtype=jnp.int32)[:, None]).astype(
        jnp.bfloat16
    )
    lmk_onehot = (tile_lmk[None, :] == jnp.arange(landmark_count, dtype=jnp.int32)[:, None]).astype(
        jnp.bfloat16
    )
    cam_count = lax.axis_size("cam")
    part_size = landmark_count // cam_count
    v_part = lax.dynamic_slice_in_dim(v_inverse, lax.axis_index("cam") * part_size, part_size, 0)
    current = jnp.einsum("bpc,bcd->bpd", probes, u_inverse, preferred_element_type=jnp.float32)
    series_sum = current
    panel = a2a_gather(current.astype(jnp.bfloat16), "lmk")
    for power_step in range(POWERS):
        tile_rows = jnp.take(panel, tile_cam, axis=0)
        forward = jnp.einsum(
            "tpc,tcl->tpl", tile_rows, couplings, preferred_element_type=jnp.float32
        )
        partial_value = onehot_sum(lmk_onehot, forward)
        landmark_part = cam_reduce(partial_value)
        landmark_part_out = jnp.einsum(
            "mpl,mlq->mpq",
            landmark_part.astype(jnp.bfloat16),
            v_part,
            preferred_element_type=jnp.float32,
        ).astype(jnp.bfloat16)
        landmark_out = cam_gather(landmark_part_out)
        picked = jnp.take(landmark_out, tile_lmk, axis=0)
        backward = jnp.einsum("tpl,tcl->tpc", picked, couplings, preferred_element_type=jnp.float32)
        camera_sum = a2a_reduce_scatter(onehot_sum(cam_onehot, backward), "lmk")
        current = jnp.einsum(
            "bpc,bcd->bpd",
            camera_sum.astype(jnp.bfloat16),
            u_inverse,
            preferred_element_type=jnp.float32,
        )
        series_sum = series_sum + current
        if power_step + 1 < POWERS:
            panel = a2a_gather(current.astype(jnp.bfloat16), "lmk")
    return series_sum


def solution(mesh):
    COLLECTIVE_IDS.clear()
    in_specs = (
        P(("cam", "lmk"), None, None),
        P(("cam", "lmk"), None, None),
        P(("cam", "lmk"), None, None),
        P("lmk", None, None),
        P(("cam", "lmk")),
        P(("cam", "lmk")),
    )
    out_specs = P(("cam", "lmk"), None, None)
    return jax.shard_map(local, mesh=mesh, in_specs=in_specs, out_specs=out_specs, check_vma=False)
```

profile of v0, /device:TPU:0, one launch (start us, length us, event | category | flops | bytes accessed | tf_op | source)
XLA Modules:
  0.0 460.2 jit_solution(2774867164622817922)
XLA Ops:
  4.0 8.8 %all-to-all-start = ((bf16[32,1,32,576]{3,2,1,0:T(8,128)(2,1)}), bf16[32,1,32,576]{3,2,1,0:T(8,128)(2,1)S(1)}, u32[]{:S(2)}, u32[]{:S(2)}) async-start(bf16[32,1,32,576]{3,2,1,0:T(8,128)(2,1)} %broadcast_in_dim.26), calls=%async_computation | async-start | bytes 2621440 | tf_op jit(solution)/shard_map/all_to_all | solution.py:92
  12.9 19.1 %all-to-all-done = bf16[32,1,32,576]{3,2,1,0:T(8,128)(2,1)S(1)} async-done(((bf16[32,1,32,576]{3,2,1,0:T(8,128)(2,1)}), bf16[32,1,32,576]{3,2,1,0:T(8,128)(2,1)S(1)}, u32[]{:S(2)}, u32[]{:S(2)}) %all-to-all-start) | async-done | bytes 1179680 | tf_op jit(solution)/shard_map/all_to_all | solution.py:92
  32.0 2.9 gather_fusion
  34.9 11.7 %subtract_convert_fusion.7 = (bf16[80,32,192]{2,1,0:T(8,128)(2,1)S(1)}, bf16[80,32,192]{2,1,0:T(8,128)(2,1)S(1)}) fusion(bf16[80,576,192]{1,2,0:T(8,128)(2,1)} %param.12, bf16[80,32,576]{2,1,0:T(8,128)(2,1)} %gather_fusion, pred[80]{0:T(512)(128)(4,1)S(1)} %compare_and_fusion.1), kind=kOutput, calls=%fused_computation.47 | convolution fusion | flops 569671680 | bytes 22610000 | tf_op jit(solution)/shard_map/tpc,tcl->tpl/dot_general | solution.py:184
  54.4 9.1 %shard_map.65 = bf16[12,32,192]{2,1,0:T(8,128)(2,1)} custom-call(bf16[12,32,192]{2,1,0:T(8,128)(2,1)} %fusion.102.x_ref), custom_call_target="tpu_custom_call" | custom-call | tf_op jit(solution)/shard_map/pallas_call | solution.py:131
  63.5 2.4 convolution_convert_fusion.3.x_ref
  65.9 8.2 %shard_map.66 = bf16[12,32,192]{2,1,0:T(8,128)(2,1)} custom-call(bf16[12,32,192]{2,1,0:T(8,128)(2,1)} %convolution_convert_fusion.3.x_ref), custom_call_target="tpu_custom_call" | custom-call | tf_op jit(solution)/shard_map/pallas_call | solution.py:131
  81.8 11.3 %subtract_convert_fusion.3 = (bf16[80,32,576]{2,1,0:T(8,128)(2,1)S(1)}, bf16[80,32,576]{2,1,0:T(8,128)(2,1)S(1)}) fusion(bf16[80,576,192]{1,2,0:T(8,128)(2,1)} %param.12, bf16[80,32,192]{2,1,0:T(8,128)(2,1)S(1)} %gather_fusion.1, pred[80]{0:T(512)(128)(4,1)S(1)} %compare_and_fusion), kind=kOutput, calls=%fused_computation.11 | convolution fusion | flops 572620800 | bytes 24576080 | tf_op jit(solution)/shard_map/tpl,tcl->tpc/dot_general | solution.py:197
  96.6 25.5 %all_to_all.40 = bf16[32,1,32,576]{3,2,1,0:T(8,128)(2,1)S(1)} all-to-all(bf16[32,1,32,576]{3,2,1,0:T(8,128)(2,1)S(1)} %copy.58), channel_id=1, replica_groups=mesh['cam'=4,'lmk'=32] {'lmk'}, dimensions={0} | all-to-all | bytes 2359296 | tf_op jit(solution)/shard_map/all_to_all | solution.py:102
  122.6 23.6 %all_to_all.41 = bf16[32,1,32,576]{3,2,1,0:T(8,128)(2,1)S(1)} all-to-all(bf16[32,1,32,576]{3,2,1,0:T(8,128)(2,1)S(1)} %broadcast_in_dim.27), channel_id=1, replica_groups=mesh['cam'=4,'lmk'=32] {'lmk'}, dimensions={0} | all-to-all | bytes 2359296 | tf_op jit(solution)/shard_map/all_to_all | solution.py:92
  146.2 2.9 gather_fusion.2
  149.1 11.5 %subtract_convert_fusion.6 = (bf16[80,32,192]{2,1,0:T(8,128)(2,1)S(1)}, bf16[80,32,192]{2,1,0:T(8,128)(2,1)S(1)}) fusion(bf16[80,576,192]{1,2,0:T(8,128)(2,1)} %param.12, bf16[80,32,576]{2,1,0:T(8,128)(2,1)} %gather_fusion.2, pred[80]{0:T(512)(128)(4,1)S(1)} %compare_and_fusion.1), kind=kOutput, calls=%fused_computation.45 | convolution fusion | flops 569671680 | bytes 22610000 | tf_op jit(solution)/shard_map/tpc,tcl->tpl/dot_general | solution.py:184
  168.4 8.8 %shard_map.69 = bf16[12,32,192]{2,1,0:T(8,128)(2,1)} custom-call(bf16[12,32,192]{2,1,0:T(8,128)(2,1)} %fusion.103.x_ref), custom_call_target="tpu_custom_call" | custom-call | tf_op jit(solution)/shard_map/pallas_call | solution.py:131
  177.2 2.4 convolution_convert_fusion.2.x_ref
  179.6 7.9 %shard_map.70 = bf16[12,32,192]{2,1,0:T(8,128)(2,1)} custom-call(bf16[12,32,192]{2,1,0:T(8,128)(2,1)} %convolution_convert_fusion.2.x_ref), custom_call_target="tpu_custom_call" | custom-call | tf_op jit(solution)/shard_map/pallas_call | solution.py:131
  195.2 11.3 %subtract_convert_fusion.2 = (bf16[80,32,576]{2,1,0:T(8,128)(2,1)S(1)}, bf16[80,32,576]{2,1,0:T(8,128)(2,1)S(1)}) fusion(bf16[80,576,192]{1,2,0:T(8,128)(2,1)} %param.12, bf16[80,32,192]{2,1,0:T(8,128)(2,1)S(1)} %gather_fusion.3, pred[80]{0:T(512)(128)(4,1)S(1)} %compare_and_fusion), kind=kOutput, calls=%fused_computation.10 | convolution fusion | flops 572620800 | bytes 24576080 | tf_op jit(solution)/shard_map/tpl,tcl->tpc/dot_general | solution.py:197
  210.0 24.4 %all_to_all.42 = bf16[32,1,32,576]{3,2,1,0:T(8,128)(2,1)S(1)} all-to-all(bf16[32,1,32,576]{3,2,1,0:T(8,128)(2,1)S(1)} %copy.66), channel_id=1, replica_groups=mesh['cam'=4,'lmk'=32] {'lmk'}, dimensions={0} | all-to-all | bytes 2359296 | tf_op jit(solution)/shard_map/all_to_all | solution.py:102
  235.0 23.3 %all_to_all.43 = bf16[32,1,32,576]{3,2,1,0:T(8,128)(2,1)S(1)} all-to-all(bf16[32,1,32,576]{3,2,1,0:T(8,128)(2,1)S(1)} %broadcast_in_dim.28), channel_id=1, replica_groups=mesh['cam'=4,'lmk'=32] {'lmk'}, dimensions={0} | all-to-all | bytes 2359296 | tf_op jit(solution)/shard_map/all_to_all | solution.py:92
  258.3 2.9 gather_fusion.4
  261.2 11.5 %subtract_convert_fusion.5 = (bf16[80,32,192]{2,1,0:T(8,128)(2,1)S(1)}, bf16[80,32,192]{2,1,0:T(8,128)(2,1)S(1)}) fusion(bf16[80,576,192]{1,2,0:T(8,128)(2,1)} %param.12, bf16[80,32,576]{2,1,0:T(8,128)(2,1)} %gather_fusion.4, pred[80]{0:T(512)(128)(4,1)S(1)} %compare_and_fusion.1), kind=kOutput, calls=%fused_computation.43 | convolution fusion | flops 569671680 | bytes 22610000 | tf_op jit(solution)/shard_map/tpc,tcl->tpl/dot_general | solution.py:184
  280.5 8.8 %shard_map.73 = bf16[12,32,192]{2,1,0:T(8,128)(2,1)} custom-call(bf16[12,32,192]{2,1,0:T(8,128)(2,1)} %fusion.104.x_ref), custom_call_target="tpu_custom_call" | custom-call | tf_op jit(solution)/shard_map/pallas_call | solution.py:131
  289.3 2.4 convolution_convert_fusion.1.x_ref
  291.7 7.9 %shard_map.74 = bf16[12,32,192]{2,1,0:T(8,128)(2,1)} custom-call(bf16[12,32,192]{2,1,0:T(8,128)(2,1)} %convolution_convert_fusion.1.x_ref), custom_call_target="tpu_custom_call" | custom-call | tf_op jit(solution)/shard_map/pallas_call | solution.py:131
  307.3 11.3 %subtract_convert_fusion.1 = (bf16[80,32,576]{2,1,0:T(8,128)(2,1)S(1)}, bf16[80,32,576]{2,1,0:T(8,128)(2,1)S(1)}) fusion(bf16[80,576,192]{1,2,0:T(8,128)(2,1)} %param.12, bf16[80,32,192]{2,1,0:T(8,128)(2,1)S(1)} %gather_fusion.5, pred[80]{0:T(512)(128)(4,1)S(1)} %compare_and_fusion), kind=kOutput, calls=%fused_computation.9 | convolution fusion | flops 572620800 | bytes 24576080 | tf_op jit(solution)/shard_map/tpl,tcl->tpc/dot_general | solution.py:197
  322.1 24.4 %all_to_all.44 = bf16[32,1,32,576]{3,2,1,0:T(8,128)(2,1)S(1)} all-to-all(bf16[32,1,32,576]{3,2,1,0:T(8,128)(2,1)S(1)} %copy.74), channel_id=1, replica_groups=mesh['cam'=4,'lmk'=32] {'lmk'}, dimensions={0} | all-to-all | bytes 2359296 | tf_op jit(solution)/shard_map/all_to_all | solution.py:102
  347.1 23.4 %all_to_all.45 = bf16[32,1,32,576]{3,2,1,0:T(8,128)(2,1)S(1)} all-to-all(bf16[32,1,32,576]{3,2,1,0:T(8,128)(2,1)S(1)} %broadcast_in_dim.29), channel_id=1, replica_groups=mesh['cam'=4,'lmk'=32] {'lmk'}, dimensions={0} | all-to-all | bytes 2359296 | tf_op jit(solution)/shard_map/all_to_all | solution.py:92
  370.5 2.9 gather_fusion.6
  373.4 11.5 %subtract_convert_fusion.4 = (bf16[80,32,192]{2,1,0:T(8,128)(2,1)S(1)}, bf16[80,32,192]{2,1,0:T(8,128)(2,1)S(1)}) fusion(bf16[80,576,192]{1,2,0:T(8,128)(2,1)} %param.12, bf16[80,32,576]{2,1,0:T(8,128)(2,1)} %gather_fusion.6, pred[80]{0:T(512)(128)(4,1)S(1)} %compare_and_fusion.1), kind=kOutput, calls=%fused_computation.41 | convolution fusion | flops 569671680 | bytes 22610000 | tf_op jit(solution)/shard_map/tpc,tcl->tpl/dot_general | solution.py:184
  392.7 8.8 %shard_map.77 = bf16[12,32,192]{2,1,0:T(8,128)(2,1)} custom-call(bf16[12,32,192]{2,1,0:T(8,128)(2,1)} %fusion.105.x_ref), custom_call_target="tpu_custom_call" | custom-call | tf_op jit(solution)/shard_map/pallas_call | solution.py:131
  403.9 7.9 %shard_map.78 = bf16[12,32,192]{2,1,0:T(8,128)(2,1)} custom-call(bf16[12,32,192]{2,1,0:T(8,128)(2,1)} %convolution_convert_fusion.x_ref), custom_call_target="tpu_custom_call" | custom-call | tf_op jit(solution)/shard_map/pallas_call | solution.py:131
  419.5 11.3 %subtract_convert_fusion = (bf16[80,32,576]{2,1,0:T(8,128)(2,1)S(1)}, bf16[80,32,576]{2,1,0:T(8,128)(2,1)S(1)}) fusion(bf16[80,576,192]{1,2,0:T(8,128)(2,1)} %param.12, bf16[80,32,192]{2,1,0:T(8,128)(2,1)S(1)} %gather_fusion.7, pred[80]{0:T(512)(128)(4,1)S(1)} %compare_and_fusion), kind=kOutput, calls=%fused_computation.8 | convolution fusion | flops 572620800 | bytes 24576080 | tf_op jit(solution)/shard_map/tpl,tcl->tpc/dot_general | solution.py:197
  434.3 24.5 %all_to_all.46 = bf16[32,1,32,576]{3,2,1,0:T(8,128)(2,1)S(1)} all-to-all(bf16[32,1,32,576]{3,2,1,0:T(8,128)(2,1)S(1)} %copy.82), channel_id=1, replica_groups=mesh['cam'=4,'lmk'=32] {'lmk'}, dimensions={0} | all-to-all | bytes 2359296 | tf_op jit(solution)/shard_map/all_to_all | solution.py:102
  (88 shorter events, 85.1 us)
Async XLA Ops:
  0.0 1.1 copy-start
  0.0 12.8 %copy-start.2 = (s32[80]{0:T(128)S(1)}, s32[80]{0:T(128)}, u32[]{:S(2)}) copy-start(s32[80]{0:T(128)} %param.15) | copy-start | bytes 964
  0.0 12.8 %copy-start.3 = (s32[80]{0:T(128)S(1)}, s32[80]{0:T(128)}, u32[]{:S(2)}) copy-start(s32[80]{0:T(128)} %param.14) | copy-start | bytes 964
  4.0 28.0 %all-to-all-start = ((bf16[32,1,32,576]{3,2,1,0:T(8,128)(2,1)}), bf16[32,1,32,576]{3,2,1,0:T(8,128)(2,1)S(1)}, u32[]{:S(2)}, u32[]{:S(2)}) async-start(bf16[32,1,32,576]{3,2,1,0:T(8,128)(2,1)} %broadcast_in_dim.26), calls=%async_computation | async-start | bytes 2621440 | tf_op jit(solution)/shard_map/all_to_all | solution.py:92
  434.3 24.8 %copy-start.1 = (f32[32,576]{1,0:T(8,128)S(1)}, f32[32,576]{1,0:T(8,128)}, u32[]{:S(2)}) copy-start(f32[32,576]{1,0:T(8,128)} %get-tuple-element.24) | copy-start | bytes 221188
where the time goes:
time: 465 us; the launch traced here: 460 us
  blocking collectives  169 us (36%)
  matrix products  125 us (27%)
  Pallas kernels  84.1 us (18%)
  other arithmetic  31.6 us (7%)
  local copies, waits for them, and re-layouts  22.2 us (5%)
  waiting for transfers between devices  19.1 us (4%)
  starting transfers between devices  8.78 us (2%)
    all_to_all x4, blocking collectives, a2a_reduce_scatter(): lax.all_to_all(chunks.astype(jnp.bfloat16), axis_name, 0, 0, tiled=False)  98.8 us
    pallas_call x16, Pallas kernels, swap(): pl.pallas_call(functools.partial(swap_kernel, partner=partner), out_shape...  84.1 us
    all_to_all x3, blocking collectives, a2a_gather(): got = lax.all_to_all(tiled, axis_name, 0, 0, tiled=False)  70.3 us
    dot_general x4, matrix products, local(): jnp.einsum('tpc,tcl->tpl', tile_rows, couplings, preferred_element_type=j...  46.3 us
    dot_general x4, matrix products, local(): jnp.einsum('tpl,tcl->tpc', picked, couplings, preferred_element_type=jnp....  45 us
    select_n x12, other arithmetic, pick(): return jnp.where(flag == 0, a, b)  19.7 us
    all_to_all x1, waiting for transfers between devices, a2a_gather(): got = lax.all_to_all(tiled, axis_name, 0, 0, tiled=False)  19.1 us
    gather x4, local copies, waits for them, and re-layouts, local(): tile_rows = jnp.take(panel, tile_cam, axis=0)  11.5 us
  transfers between devices with their start and end apart: 1, of which 1 were waited for; matrix products, arithmetic and copies ran while one was open for 0% of the time, Pallas kernels for 0%

commit v1 on v0

--- a/solution.py
+++ b/solution.py
@@ -138,29 +138,36 @@
     )(x)
 
 
-def pick(flag, a, b):
-    return jnp.where(flag == 0, a, b)
+def take(stack, index, axis):
+    return lax.dynamic_index_in_dim(stack, index, axis=axis, keepdims=False)
 
 
 def cam_reduce(partial_value):
     cam = lax.axis_index("cam")
     core, high = cam % 2, cam // 2
     chunks = partial_value.reshape((2, 2, partial_value.shape[0] // 4) + partial_value.shape[1:])
-    mine = pick(core, chunks[:, 0], chunks[:, 1])
-    theirs = pick(core, chunks[:, 1], chunks[:, 0])
+    mine = take(chunks, core, 1)
+    theirs = take(chunks, 1 - core, 1)
     chip = mine + swap(theirs.astype(jnp.bfloat16), 1).astype(jnp.float32)
-    keep = pick(high, chip[0], chip[1])
-    send = pick(high, chip[1], chip[0])
+    keep = take(chip, high, 0)
+    send = take(chip, 1 - high, 0)
     return keep + swap(send.astype(jnp.bfloat16), 2).astype(jnp.float32)
+
+
+def place(block, other, index, axis):
+    both = jnp.stack([other, other], axis=axis)
+    starts = [0] * both.ndim
+    starts[axis] = index
+    return lax.dynamic_update_slice(both, jnp.expand_dims(block, axis), starts)
 
 
 def cam_gather(block):
     cam = lax.axis_index("cam")
     core, high = cam % 2, cam // 2
     other = swap(block, 2)
-    pair = pick(high, jnp.stack([block, other]), jnp.stack([other, block]))
+    pair = place(block, other, high, 0)
     other_pair = swap(pair, 1)
-    full = pick(core, jnp.stack([pair, other_pair], axis=1), jnp.stack([other_pair, pair], axis=1))
+    full = place(pair, other_pair, core, 1)
     return full.reshape((4 * block.shape[0],) + block.shape[1:])
 
 
@@ -177,9 +184,9 @@
     part_size = landmark_count // cam_count
     v_part = lax.dynamic_slice_in_dim(v_inverse, lax.axis_index("cam") * part_size, part_size, 0)
     current = jnp.einsum("bpc,bcd->bpd", probes, u_inverse, preferred_element_type=jnp.float32)
-    series_sum = current
-    panel = a2a_gather(current.astype(jnp.bfloat16), "lmk")
-    for power_step in range(POWERS):
+    def power(step, carry):
+        current, series_sum = carry
+        panel = a2a_gather(current.astype(jnp.bfloat16), "lmk")
         tile_rows = jnp.take(panel, tile_cam, axis=0)
         forward = jnp.einsum(
             "tpc,tcl->tpl", tile_rows, couplings, preferred_element_type=jnp.float32
@@ -202,9 +209,9 @@
             u_inverse,
             preferred_element_type=jnp.float32,
         )
-        series_sum = series_sum + current
-        if power_step + 1 < POWERS:
-            panel = a2a_gather(current.astype(jnp.bfloat16), "lmk")
+        return current, series_sum + current
+
+    _, series_sum = lax.fori_loop(0, POWERS, power, (current, current))
     return series_sum
 
 

time: 465 us -> 473 us (1.017)
  blocking collectives: 169 us -> 0 us
  waiting for transfers between devices: 19.1 us -> 152 us
  starting transfers between devices: 8.78 us -> 43.6 us
  local copies, waits for them, and re-layouts: 22.2 us -> 53.1 us
  other arithmetic: 31.6 us -> 14.9 us
    all_to_all x7 -> x0, blocking collectives: 169 us -> none  [the longest x4 98.8 us: a2a_reduce_scatter(): lax.all_to_all(chunks.astype(jnp.bfloat16), axis_name, 0, 0, tiled=False)]
    all_to_all x0 -> x4, waiting for transfers between devices: none -> 78 us  [a2a_reduce_scatter(): lax.all_to_all(chunks.astype(jnp.bfloat16), axis_name, 0, 0, tiled=False)]
    all_to_all x1 -> x4, waiting for transfers between devices: 19.1 us -> 73.8 us  [a2a_gather(): got = lax.all_to_all(tiled, axis_name, 0, 0, tiled=False)]
    select_n x14 -> x4, other arithmetic: 19.7 us -> 0.02 us  [power(): tile_rows = jnp.take(panel, tile_cam, axis=0)]
    all_to_all x0 -> x4, starting transfers between devices: none -> 19.4 us  [a2a_reduce_scatter(): lax.all_to_all(chunks.astype(jnp.bfloat16), axis_name, 0, 0, tiled=False)]
    all_to_all x1 -> x4, starting transfers between devices: 8.78 us -> 24.2 us  [a2a_gather(): got = lax.all_to_all(tiled, axis_name, 0, 0, tiled=False)]
    another operation x0 -> x8, other arithmetic: none -> 9.47 us  [place(): both = jnp.stack([other, other], axis=axis)]
    dynamic_update_slice x0 -> x12, local copies, waits for them, and re-layouts: none -> 8.12 us  [place(): return lax.dynamic_update_slice(both, jnp.expand_dims(block, axis), starts)]
  transfers between devices with their start and end apart: 1 -> 8, of which waited for: 1 -> 8; matrix products, arithmetic and copies ran while one was open for 0% -> 0% of each run, Pallas kernels for 0% -> 0%
where the time goes in v1:
time: 473 us; the launch traced here: 471 us
  waiting for transfers between devices  152 us (32%)
  matrix products  122 us (26%)
  Pallas kernels  84.1 us (18%)
  local copies, waits for them, and re-layouts  53.1 us (11%)
  starting transfers between devices  43.6 us (9%)
  other arithmetic  14.9 us (3%)
    pallas_call x16, Pallas kernels, swap(): pl.pallas_call(functools.partial(swap_kernel, partner=partner), out_shape...  84.1 us
    all_to_all x4, waiting for transfers between devices, a2a_reduce_scatter(): lax.all_to_all(chunks.astype(jnp.bfloat16), axis_name, 0, 0, tiled=False)  78 us
    all_to_all x4, waiting for transfers between devices, a2a_gather(): got = lax.all_to_all(tiled, axis_name, 0, 0, tiled=False)  73.8 us
    dot_general x4, matrix products, power(): jnp.einsum('tpl,tcl->tpc', picked, couplings, preferred_element_type=jnp....  45.3 us
    dot_general x4, matrix products, power(): jnp.einsum('tpc,tcl->tpl', tile_rows, couplings, preferred_element_type=j...  44.3 us
    all_to_all x4, starting transfers between devices, a2a_gather(): got = lax.all_to_all(tiled, axis_name, 0, 0, tiled=False)  24.2 us
    all_to_all x4, starting transfers between devices, a2a_reduce_scatter(): lax.all_to_all(chunks.astype(jnp.bfloat16), axis_name, 0, 0, tiled=False)  19.4 us
    dot_general x8, matrix products, onehot_sum(): jnp.einsum('st,tpx->spx', selected, upper, preferred_element_type=jnp.flo...  10.8 us
  transfers between devices with their start and end apart: 8, of which 8 were waited for; matrix products, arithmetic and copies ran while one was open for 0% of the time, Pallas kernels for 0%

profile of v1, /device:TPU:0, one launch (start us, length us, event | category | flops | bytes accessed | tf_op | source)
XLA Modules:
  0.0 470.8 jit_solution(5486579188324859735)
XLA Ops:
  5.2 464.9 %while.17 = (s32[]{:T(128)}, bf16[1,32,576]{2,1,0:T(8,128)(2,1)S(1)}, f32[1,32,576]{2,1,0:T(8,128)S(1)}, s32[80]{0:T(128)S(1)}, s32[80]{0:T(128)S(1)}, /*index=5...) while((s32[]{:T(128)}, ...), condition=%wide.region_2.3_spmd.clone.clone, body=%wide.region_0.2_spmd.clone.clone.sunk | while | flops 1478097408 | bytes 104027504 | solution.py:214
  6.4 8.8 %all-to-all-start = ((bf16[32,1,32,576]{3,2,1,0:T(8,128)(2,1)}), bf16[32,1,32,576]{3,2,1,0:T(8,128)(2,1)S(1)}, u32[]{:S(2)}, u32[]{:S(2)}) async-start(bf16[32,1,32,576]{3,2,1,0:T(8,128)(2,1)} %broadcast_in_dim.115), calls=%async_computation | async-start | bytes 2621440 | tf_op jit(solution)/shard_map/while/body/eval_jaxpr/all_to_all | solution.py:92
  15.3 19.1 %all-to-all-done = bf16[32,1,32,576]{3,2,1,0:T(8,128)(2,1)S(1)} async-done(((bf16[32,1,32,576]{3,2,1,0:T(8,128)(2,1)}), bf16[32,1,32,576]{3,2,1,0:T(8,128)(2,1)S(1)}, u32[]{:S(2)}, u32[]{:S(2)}) %all-to-all-start) | async-done | bytes 1179680 | tf_op jit(solution)/shard_map/while/body/eval_jaxpr/all_to_all | solution.py:92
  38.1 11.1 %subtract_convert_fusion.4 = (bf16[80,32,192]{2,1,0:T(8,128)(2,1)S(1)}, bf16[80,32,192]{2,1,0:T(8,128)(2,1)S(1)}) fusion(bf16[80,576,192]{1,2,0:T(8,128)(2,1)} %get-tuple-element.354, bf16[80,32,576]{2,1,0:T(8,128)(2,1)S(1)} %gather_fusion, pred[80]{0:T(512)(128)(4,1)S(1)} %get-tuple-element.308), kind=kOutput, calls=%fused_computation.13.clone.1 | convolution fusion | flops 569671680 | bytes 22610000 | tf_op jit(solution)/shard_map/while/body/eval_jaxpr/tpc,tcl->tpl/dot_general | solution.py:191
  56.9 9.1 %eval_jaxpr.21 = bf16[12,32,192]{2,1,0:T(8,128)(2,1)} custom-call(bf16[12,32,192]{2,1,0:T(8,128)(2,1)} %fusion.89.x_ref), custom_call_target="tpu_custom_call" | custom-call | tf_op jit(solution)/shard_map/while/body/eval_jaxpr/pallas_call | solution.py:131
  68.4 8.2 %eval_jaxpr.22 = bf16[12,32,192]{2,1,0:T(8,128)(2,1)} custom-call(bf16[12,32,192]{2,1,0:T(8,128)(2,1)} %convolution_convert_fusion.2.x_ref), custom_call_target="tpu_custom_call" | custom-call | tf_op jit(solution)/shard_map/while/body/eval_jaxpr/pallas_call | solution.py:131
  84.6 11.3 %subtract_convert_fusion.5 = (bf16[80,32,576]{2,1,0:T(8,128)(2,1)S(1)}, bf16[80,32,576]{2,1,0:T(8,128)(2,1)S(1)}) fusion(bf16[80,576,192]{1,2,0:T(8,128)(2,1)} %get-tuple-element.354, bf16[80,32,192]{2,1,0:T(8,128)(2,1)S(1)} %gather_fusion.1, pred[80]{0:T(512)(128)(4,1)S(1)} %get-tuple-element.312), kind=kOutput, calls=%fused_computation.4.clone.1 | convolution fusion | flops 572620800 | bytes 24576080 | tf_op jit(solution)/shard_map/while/body/eval_jaxpr/tpl,tcl->tpc/dot_general | solution.py:204
  100.5 5.0 %all-to-all-start.1 = ((bf16[32,1,32,576]{3,2,1,0:T(8,128)(2,1)}), bf16[32,1,32,576]{3,2,1,0:T(8,128)(2,1)S(1)}, u32[]{:S(2)}, u32[]{:S(2)}) async-start(bf16[32,1,32,576]{3,2,1,0:T(8,128)(2,1)} %copy.52), calls=%async_computation.1 | async-start | bytes 2621440 | tf_op jit(solution)/shard_map/while/body/eval_jaxpr/all_to_all | solution.py:102
  105.6 19.5 %all-to-all-done.1 = bf16[32,1,32,576]{3,2,1,0:T(8,128)(2,1)S(1)} async-done(((bf16[32,1,32,576]{3,2,1,0:T(8,128)(2,1)}), bf16[32,1,32,576]{3,2,1,0:T(8,128)(2,1)S(1)}, u32[]{:S(2)}, u32[]{:S(2)}) %all-to-all-start.1) | async-done | bytes 1179680 | tf_op jit(solution)/shard_map/while/body/eval_jaxpr/all_to_all | solution.py:102
  126.7 5.1 %all-to-all-start = ((bf16[32,1,32,576]{3,2,1,0:T(8,128)(2,1)}), bf16[32,1,32,576]{3,2,1,0:T(8,128)(2,1)S(1)}, u32[]{:S(2)}, u32[]{:S(2)}) async-start(bf16[32,1,32,576]{3,2,1,0:T(8,128)(2,1)} %broadcast_in_dim.115), calls=%async_computation | async-start | bytes 2621440 | tf_op jit(solution)/shard_map/while/body/eval_jaxpr/all_to_all | solution.py:92
  132.0 18.2 %all-to-all-done = bf16[32,1,32,576]{3,2,1,0:T(8,128)(2,1)S(1)} async-done(((bf16[32,1,32,576]{3,2,1,0:T(8,128)(2,1)}), bf16[32,1,32,576]{3,2,1,0:T(8,128)(2,1)S(1)}, u32[]{:S(2)}, u32[]{:S(2)}) %all-to-all-start) | async-done | bytes 1179680 | tf_op jit(solution)/shard_map/while/body/eval_jaxpr/all_to_all | solution.py:92
  153.8 11.1 %subtract_convert_fusion.4 = (bf16[80,32,192]{2,1,0:T(8,128)(2,1)S(1)}, bf16[80,32,192]{2,1,0:T(8,128)(2,1)S(1)}) fusion(bf16[80,576,192]{1,2,0:T(8,128)(2,1)} %get-tuple-element.354, bf16[80,32,576]{2,1,0:T(8,128)(2,1)S(1)} %gather_fusion, pred[80]{0:T(512)(128)(4,1)S(1)} %get-tuple-element.308), kind=kOutput, calls=%fused_computation.13.clone.1 | convolution fusion | flops 569671680 | bytes 22610000 | tf_op jit(solution)/shard_map/while/body/eval_jaxpr/tpc,tcl->tpl/dot_general | solution.py:191
  172.6 8.8 %eval_jaxpr.21 = bf16[12,32,192]{2,1,0:T(8,128)(2,1)} custom-call(bf16[12,32,192]{2,1,0:T(8,128)(2,1)} %fusion.89.x_ref), custom_call_target="tpu_custom_call" | custom-call | tf_op jit(solution)/shard_map/while/body/eval_jaxpr/pallas_call | solution.py:131
  183.8 7.9 %eval_jaxpr.22 = bf16[12,32,192]{2,1,0:T(8,128)(2,1)} custom-call(bf16[12,32,192]{2,1,0:T(8,128)(2,1)} %convolution_convert_fusion.2.x_ref), custom_call_target="tpu_custom_call" | custom-call | tf_op jit(solution)/shard_map/while/body/eval_jaxpr/pallas_call | solution.py:131
  199.7 11.3 %subtract_convert_fusion.5 = (bf16[80,32,576]{2,1,0:T(8,128)(2,1)S(1)}, bf16[80,32,576]{2,1,0:T(8,128)(2,1)S(1)}) fusion(bf16[80,576,192]{1,2,0:T(8,128)(2,1)} %get-tuple-element.354, bf16[80,32,192]{2,1,0:T(8,128)(2,1)S(1)} %gather_fusion.1, pred[80]{0:T(512)(128)(4,1)S(1)} %get-tuple-element.312), kind=kOutput, calls=%fused_computation.4.clone.1 | convolution fusion | flops 572620800 | bytes 24576080 | tf_op jit(solution)/shard_map/while/body/eval_jaxpr/tpl,tcl->tpc/dot_general | solution.py:204
  215.7 4.8 %all-to-all-start.1 = ((bf16[32,1,32,576]{3,2,1,0:T(8,128)(2,1)}), bf16[32,1,32,576]{3,2,1,0:T(8,128)(2,1)S(1)}, u32[]{:S(2)}, u32[]{:S(2)}) async-start(bf16[32,1,32,576]{3,2,1,0:T(8,128)(2,1)} %copy.52), calls=%async_computation.1 | async-start | bytes 2621440 | tf_op jit(solution)/shard_map/while/body/eval_jaxpr/all_to_all | solution.py:102
  220.5 19.5 %all-to-all-done.1 = bf16[32,1,32,576]{3,2,1,0:T(8,128)(2,1)S(1)} async-done(((bf16[32,1,32,576]{3,2,1,0:T(8,128)(2,1)}), bf16[32,1,32,576]{3,2,1,0:T(8,128)(2,1)S(1)}, u32[]{:S(2)}, u32[]{:S(2)}) %all-to-all-start.1) | async-done | bytes 1179680 | tf_op jit(solution)/shard_map/while/body/eval_jaxpr/all_to_all | solution.py:102
  241.6 5.1 %all-to-all-start = ((bf16[32,1,32,576]{3,2,1,0:T(8,128)(2,1)}), bf16[32,1,32,576]{3,2,1,0:T(8,128)(2,1)S(1)}, u32[]{:S(2)}, u32[]{:S(2)}) async-start(bf16[32,1,32,576]{3,2,1,0:T(8,128)(2,1)} %broadcast_in_dim.115), calls=%async_computation | async-start | bytes 2621440 | tf_op jit(solution)/shard_map/while/body/eval_jaxpr/all_to_all | solution.py:92
  246.8 18.2 %all-to-all-done = bf16[32,1,32,576]{3,2,1,0:T(8,128)(2,1)S(1)} async-done(((bf16[32,1,32,576]{3,2,1,0:T(8,128)(2,1)}), bf16[32,1,32,576]{3,2,1,0:T(8,128)(2,1)S(1)}, u32[]{:S(2)}, u32[]{:S(2)}) %all-to-all-start) | async-done | bytes 1179680 | tf_op jit(solution)/shard_map/while/body/eval_jaxpr/all_to_all | solution.py:92
  268.7 11.1 %subtract_convert_fusion.4 = (bf16[80,32,192]{2,1,0:T(8,128)(2,1)S(1)}, bf16[80,32,192]{2,1,0:T(8,128)(2,1)S(1)}) fusion(bf16[80,576,192]{1,2,0:T(8,128)(2,1)} %get-tuple-element.354, bf16[80,32,576]{2,1,0:T(8,128)(2,1)S(1)} %gather_fusion, pred[80]{0:T(512)(128)(4,1)S(1)} %get-tuple-element.308), kind=kOutput, calls=%fused_computation.13.clone.1 | convolution fusion | flops 569671680 | bytes 22610000 | tf_op jit(solution)/shard_map/while/body/eval_jaxpr/tpc,tcl->tpl/dot_general | solution.py:191
  287.5 8.8 %eval_jaxpr.21 = bf16[12,32,192]{2,1,0:T(8,128)(2,1)} custom-call(bf16[12,32,192]{2,1,0:T(8,128)(2,1)} %fusion.89.x_ref), custom_call_target="tpu_custom_call" | custom-call | tf_op jit(solution)/shard_map/while/body/eval_jaxpr/pallas_call | solution.py:131
  298.7 7.9 %eval_jaxpr.22 = bf16[12,32,192]{2,1,0:T(8,128)(2,1)} custom-call(bf16[12,32,192]{2,1,0:T(8,128)(2,1)} %convolution_convert_fusion.2.x_ref), custom_call_target="tpu_custom_call" | custom-call | tf_op jit(solution)/shard_map/while/body/eval_jaxpr/pallas_call | solution.py:131
  314.6 11.3 %subtract_convert_fusion.5 = (bf16[80,32,576]{2,1,0:T(8,128)(2,1)S(1)}, bf16[80,32,576]{2,1,0:T(8,128)(2,1)S(1)}) fusion(bf16[80,576,192]{1,2,0:T(8,128)(2,1)} %get-tuple-element.354, bf16[80,32,192]{2,1,0:T(8,128)(2,1)S(1)} %gather_fusion.1, pred[80]{0:T(512)(128)(4,1)S(1)} %get-tuple-element.312), kind=kOutput, calls=%fused_computation.4.clone.1 | convolution fusion | flops 572620800 | bytes 24576080 | tf_op jit(solution)/shard_map/while/body/eval_jaxpr/tpl,tcl->tpc/dot_general | solution.py:204
  335.3 19.5 %all-to-all-done.1 = bf16[32,1,32,576]{3,2,1,0:T(8,128)(2,1)S(1)} async-done(((bf16[32,1,32,576]{3,2,1,0:T(8,128)(2,1)}), bf16[32,1,32,576]{3,2,1,0:T(8,128)(2,1)S(1)}, u32[]{:S(2)}, u32[]{:S(2)}) %all-to-all-start.1) | async-done | bytes 1179680 | tf_op jit(solution)/shard_map/while/body/eval_jaxpr/all_to_all | solution.py:102
  356.5 5.1 %all-to-all-start = ((bf16[32,1,32,576]{3,2,1,0:T(8,128)(2,1)}), bf16[32,1,32,576]{3,2,1,0:T(8,128)(2,1)S(1)}, u32[]{:S(2)}, u32[]{:S(2)}) async-start(bf16[32,1,32,576]{3,2,1,0:T(8,128)(2,1)} %broadcast_in_dim.115), calls=%async_computation | async-start | bytes 2621440 | tf_op jit(solution)/shard_map/while/body/eval_jaxpr/all_to_all | solution.py:92
  361.7 18.2 %all-to-all-done = bf16[32,1,32,576]{3,2,1,0:T(8,128)(2,1)S(1)} async-done(((bf16[32,1,32,576]{3,2,1,0:T(8,128)(2,1)}), bf16[32,1,32,576]{3,2,1,0:T(8,128)(2,1)S(1)}, u32[]{:S(2)}, u32[]{:S(2)}) %all-to-all-start) | async-done | bytes 1179680 | tf_op jit(solution)/shard_map/while/body/eval_jaxpr/all_to_all | solution.py:92
  383.5 11.1 %subtract_convert_fusion.4 = (bf16[80,32,192]{2,1,0:T(8,128)(2,1)S(1)}, bf16[80,32,192]{2,1,0:T(8,128)(2,1)S(1)}) fusion(bf16[80,576,192]{1,2,0:T(8,128)(2,1)} %get-tuple-element.354, bf16[80,32,576]{2,1,0:T(8,128)(2,1)S(1)} %gather_fusion, pred[80]{0:T(512)(128)(4,1)S(1)} %get-tuple-element.308), kind=kOutput, calls=%fused_computation.13.clone.1 | convolution fusion | flops 569671680 | bytes 22610000 | tf_op jit(solution)/shard_map/while/body/eval_jaxpr/tpc,tcl->tpl/dot_general | solution.py:191
  402.3 8.8 %eval_jaxpr.21 = bf16[12,32,192]{2,1,0:T(8,128)(2,1)} custom-call(bf16[12,32,192]{2,1,0:T(8,128)(2,1)} %fusion.89.x_ref), custom_call_target="tpu_custom_call" | custom-call | tf_op jit(solution)/shard_map/while/body/eval_jaxpr/pallas_call | solution.py:131
  413.5 7.9 %eval_jaxpr.22 = bf16[12,32,192]{2,1,0:T(8,128)(2,1)} custom-call(bf16[12,32,192]{2,1,0:T(8,128)(2,1)} %convolution_convert_fusion.2.x_ref), custom_call_target="tpu_custom_call" | custom-call | tf_op jit(solution)/shard_map/while/body/eval_jaxpr/pallas_call | solution.py:131
  429.4 11.3 %subtract_convert_fusion.5 = (bf16[80,32,576]{2,1,0:T(8,128)(2,1)S(1)}, bf16[80,32,576]{2,1,0:T(8,128)(2,1)S(1)}) fusion(bf16[80,576,192]{1,2,0:T(8,128)(2,1)} %get-tuple-element.354, bf16[80,32,192]{2,1,0:T(8,128)(2,1)S(1)} %gather_fusion.1, pred[80]{0:T(512)(128)(4,1)S(1)} %get-tuple-element.312), kind=kOutput, calls=%fused_computation.4.clone.1 | convolution fusion | flops 572620800 | bytes 24576080 | tf_op jit(solution)/shard_map/while/body/eval_jaxpr/tpl,tcl->tpc/dot_general | solution.py:204
  445.4 4.8 %all-to-all-start.1 = ((bf16[32,1,32,576]{3,2,1,0:T(8,128)(2,1)}), bf16[32,1,32,576]{3,2,1,0:T(8,128)(2,1)S(1)}, u32[]{:S(2)}, u32[]{:S(2)}) async-start(bf16[32,1,32,576]{3,2,1,0:T(8,128)(2,1)} %copy.52), calls=%async_computation.1 | async-start | bytes 2621440 | tf_op jit(solution)/shard_map/while/body/eval_jaxpr/all_to_all | solution.py:102
  450.2 19.5 %all-to-all-done.1 = bf16[32,1,32,576]{3,2,1,0:T(8,128)(2,1)S(1)} async-done(((bf16[32,1,32,576]{3,2,1,0:T(8,128)(2,1)}), bf16[32,1,32,576]{3,2,1,0:T(8,128)(2,1)S(1)}, u32[]{:S(2)}, u32[]{:S(2)}) %all-to-all-start.1) | async-done | bytes 1179680 | tf_op jit(solution)/shard_map/while/body/eval_jaxpr/all_to_all | solution.py:102
  (144 shorter events, 122.3 us)
Async XLA Ops:
  0.0 0.8 copy-start
  0.8 4.4 copy-start.7
  0.8 4.4 copy-start.8
  2.2 0.6 copy-start.4
  2.8 2.4 copy-start.5
  6.4 28.0 %all-to-all-start = ((bf16[32,1,32,576]{3,2,1,0:T(8,128)(2,1)}), bf16[32,1,32,576]{3,2,1,0:T(8,128)(2,1)S(1)}, u32[]{:S(2)}, u32[]{:S(2)}) async-start(bf16[32,1,32,576]{3,2,1,0:T(8,128)(2,1)} %broadcast_in_dim.115), calls=%async_computation | async-start | bytes 2621440 | tf_op jit(solution)/shard_map/while/body/eval_jaxpr/all_to_all | solution.py:92
  34.5 1.1 copy-start.1
  78.7 0.8 copy-start.2
  100.5 24.7 %copy-start.3 = (bf16[1,576,576]{2,1,0:T(8,128)(2,1)S(1)}, bf16[1,576,576]{2,1,0:T(8,128)(2,1)}, u32[]{:S(2)}) copy-start(bf16[1,576,576]{2,1,0:T(8,128)(2,1)} %get-tuple-element.356) | copy-start | bytes 1990660 | tf_op jit(solution)/shard_map/while
  100.5 24.5 %all-to-all-start.1 = ((bf16[32,1,32,576]{3,2,1,0:T(8,128)(2,1)}), bf16[32,1,32,576]{3,2,1,0:T(8,128)(2,1)S(1)}, u32[]{:S(2)}, u32[]{:S(2)}) async-start(bf16[32,1,32,576]{3,2,1,0:T(8,128)(2,1)} %copy.52), calls=%async_computation.1 | async-start | bytes 2621440 | tf_op jit(solution)/shard_map/while/body/eval_jaxpr/all_to_all | solution.py:102
  126.7 23.5 %all-to-all-start = ((bf16[32,1,32,576]{3,2,1,0:T(8,128)(2,1)}), bf16[32,1,32,576]{3,2,1,0:T(8,128)(2,1)S(1)}, u32[]{:S(2)}, u32[]{:S(2)}) async-start(bf16[32,1,32,576]{3,2,1,0:T(8,128)(2,1)} %broadcast_in_dim.115), calls=%async_computation | async-start | bytes 2621440 | tf_op jit(solution)/shard_map/while/body/eval_jaxpr/all_to_all | solution.py:92
  150.2 1.1 copy-start.1
  193.8 0.8 copy-start.2
  215.7 24.5 %copy-start.3 = (bf16[1,576,576]{2,1,0:T(8,128)(2,1)S(1)}, bf16[1,576,576]{2,1,0:T(8,128)(2,1)}, u32[]{:S(2)}) copy-start(bf16[1,576,576]{2,1,0:T(8,128)(2,1)} %get-tuple-element.356) | copy-start | bytes 1990660 | tf_op jit(solution)/shard_map/while
  215.7 24.3 %all-to-all-start.1 = ((bf16[32,1,32,576]{3,2,1,0:T(8,128)(2,1)}), bf16[32,1,32,576]{3,2,1,0:T(8,128)(2,1)S(1)}, u32[]{:S(2)}, u32[]{:S(2)}) async-start(bf16[32,1,32,576]{3,2,1,0:T(8,128)(2,1)} %copy.52), calls=%async_computation.1 | async-start | bytes 2621440 | tf_op jit(solution)/shard_map/while/body/eval_jaxpr/all_to_all | solution.py:102
  241.6 23.5 %all-to-all-start = ((bf16[32,1,32,576]{3,2,1,0:T(8,128)(2,1)}), bf16[32,1,32,576]{3,2,1,0:T(8,128)(2,1)S(1)}, u32[]{:S(2)}, u32[]{:S(2)}) async-start(bf16[32,1,32,576]{3,2,1,0:T(8,128)(2,1)} %broadcast_in_dim.115), calls=%async_computation | async-start | bytes 2621440 | tf_op jit(solution)/shard_map/while/body/eval_jaxpr/all_to_all | solution.py:92
  265.1 1.1 copy-start.1
  308.6 0.8 copy-start.2
  330.5 24.5 %copy-start.3 = (bf16[1,576,576]{2,1,0:T(8,128)(2,1)S(1)}, bf16[1,576,576]{2,1,0:T(8,128)(2,1)}, u32[]{:S(2)}) copy-start(bf16[1,576,576]{2,1,0:T(8,128)(2,1)} %get-tuple-element.356) | copy-start | bytes 1990660 | tf_op jit(solution)/shard_map/while
  330.5 24.3 %all-to-all-start.1 = ((bf16[32,1,32,576]{3,2,1,0:T(8,128)(2,1)}), bf16[32,1,32,576]{3,2,1,0:T(8,128)(2,1)S(1)}, u32[]{:S(2)}, u32[]{:S(2)}) async-start(bf16[32,1,32,576]{3,2,1,0:T(8,128)(2,1)} %copy.52), calls=%async_computation.1 | async-start | bytes 2621440 | tf_op jit(solution)/shard_map/while/body/eval_jaxpr/all_to_all | solution.py:102
  356.5 23.5 %all-to-all-start = ((bf16[32,1,32,576]{3,2,1,0:T(8,128)(2,1)}), bf16[32,1,32,576]{3,2,1,0:T(8,128)(2,1)S(1)}, u32[]{:S(2)}, u32[]{:S(2)}) async-start(bf16[32,1,32,576]{3,2,1,0:T(8,128)(2,1)} %broadcast_in_dim.115), calls=%async_computation | async-start | bytes 2621440 | tf_op jit(solution)/shard_map/while/body/eval_jaxpr/all_to_all | solution.py:92
  379.9 1.1 copy-start.1
  423.5 0.8 copy-start.2
  445.4 24.5 %copy-start.3 = (bf16[1,576,576]{2,1,0:T(8,128)(2,1)S(1)}, bf16[1,576,576]{2,1,0:T(8,128)(2,1)}, u32[]{:S(2)}) copy-start(bf16[1,576,576]{2,1,0:T(8,128)(2,1)} %get-tuple-element.356) | copy-start | bytes 1990660 | tf_op jit(solution)/shard_map/while
  445.4 24.3 %all-to-all-start.1 = ((bf16[32,1,32,576]{3,2,1,0:T(8,128)(2,1)}), bf16[32,1,32,576]{3,2,1,0:T(8,128)(2,1)S(1)}, u32[]{:S(2)}, u32[]{:S(2)}) async-start(bf16[32,1,32,576]{3,2,1,0:T(8,128)(2,1)} %copy.52), calls=%async_computation.1 | async-start | bytes 2621440 | tf_op jit(solution)/shard_map/while/body/eval_jaxpr/all_to_all | solution.py:102
  470.1 0.6 copy-start.6

commit v2 on v0

--- a/solution.py
+++ b/solution.py
@@ -154,13 +154,58 @@
     return keep + swap(send.astype(jnp.bfloat16), 2).astype(jnp.float32)
 
 
+def cam_gather_kernel(x_ref, o_ref, send_sem, recv_sem, local_sem):
+    cam = lax.axis_index("cam")
+    lmk = lax.axis_index("lmk")
+    core_peer, high_peer = cam ^ 1, cam ^ 2
+    barrier = pltpu.get_barrier_semaphore()
+    for peer in (core_peer, high_peer):
+        pl.semaphore_signal(barrier, inc=1, device_id=(peer, lmk), device_id_type=MESH)
+    pl.semaphore_wait(barrier, 2)
+
+    def remote(src, dst, slot, peer):
+        return pltpu.make_async_remote_copy(
+            src_ref=src,
+            dst_ref=dst,
+            send_sem=send_sem.at[slot],
+            recv_sem=recv_sem.at[slot],
+            device_id=(peer, lmk),
+            device_id_type=MESH,
+        )
+
+    local = pltpu.make_async_copy(x_ref, o_ref.at[cam], local_sem)
+    local.start()
+    to_high = remote(x_ref, o_ref.at[cam], 0, high_peer)
+    to_high.start()
+    to_core = remote(x_ref, o_ref.at[cam], 1, core_peer)
+    to_core.start()
+    remote(o_ref.at[high_peer], o_ref.at[high_peer], 0, high_peer).wait_recv()
+    relay = remote(o_ref.at[high_peer], o_ref.at[high_peer], 2, core_peer)
+    relay.start()
+    local.wait()
+    to_high.wait_send()
+    to_core.wait_send()
+    relay.wait_send()
+    remote(o_ref.at[core_peer], o_ref.at[core_peer], 1, core_peer).wait_recv()
+    remote(o_ref.at[cam ^ 3], o_ref.at[cam ^ 3], 2, core_peer).wait_recv()
+
+
 def cam_gather(block):
-    cam = lax.axis_index("cam")
-    core, high = cam % 2, cam // 2
-    other = swap(block, 2)
-    pair = pick(high, jnp.stack([block, other]), jnp.stack([other, block]))
-    other_pair = swap(pair, 1)
-    full = pick(core, jnp.stack([pair, other_pair], axis=1), jnp.stack([other_pair, pair], axis=1))
+    key = ("cam_gather", block.shape, str(block.dtype))
+    if key not in COLLECTIVE_IDS:
+        COLLECTIVE_IDS[key] = len(COLLECTIVE_IDS)
+    full = pl.pallas_call(
+        cam_gather_kernel,
+        out_shape=jax.ShapeDtypeStruct((4,) + block.shape, block.dtype),
+        in_specs=[pl.BlockSpec(memory_space=pl.ANY)],
+        out_specs=pl.BlockSpec(memory_space=pl.ANY),
+        scratch_shapes=[
+            pltpu.SemaphoreType.DMA((3,)),
+            pltpu.SemaphoreType.DMA((3,)),
+            pltpu.SemaphoreType.DMA,
+        ],
+        compiler_params=pltpu.CompilerParams(collective_id=COLLECTIVE_IDS[key], has_side_effects=True),
+    )(block)
     return full.reshape((4 * block.shape[0],) + block.shape[1:])
 
 

time: 465 us -> 449 us (0.966)
  other arithmetic: 31.6 us -> 11.9 us
    pallas_call x16 -> x8, Pallas kernels: 84.1 us -> 43.8 us  [swap(): pl.pallas_call(functools.partial(swap_kernel, partner=partner), out_shape...]
    pallas_call x0 -> x4, Pallas kernels: none -> 39 us  [cam_gather(): pl.pallas_call(cam_gather_kernel, out_shape=jax.ShapeDtypeStruct((4,) + b...]
    select_n x12 -> x0, other arithmetic: 19.7 us -> none  [pick(): return jnp.where(flag == 0, a, b)]
where the time goes in v2:
time: 449 us; the launch traced here: 445 us
  blocking collectives  170 us (38%)
  matrix products  125 us (28%)
  Pallas kernels  82.8 us (18%)
  local copies, waits for them, and re-layouts  26.7 us (6%)
  waiting for transfers between devices  19.1 us (4%)
  other arithmetic  11.9 us (3%)
  starting transfers between devices  8.78 us (2%)
    all_to_all x4, blocking collectives, a2a_reduce_scatter(): lax.all_to_all(chunks.astype(jnp.bfloat16), axis_name, 0, 0, tiled=False)  99.4 us
    all_to_all x3, blocking collectives, a2a_gather(): got = lax.all_to_all(tiled, axis_name, 0, 0, tiled=False)  71 us
    dot_general x4, matrix products, local(): jnp.einsum('tpc,tcl->tpl', tile_rows, couplings, preferred_element_type=j...  46.3 us
    dot_general x4, matrix products, local(): jnp.einsum('tpl,tcl->tpc', picked, couplings, preferred_element_type=jnp....  45 us
    pallas_call x8, Pallas kernels, swap(): pl.pallas_call(functools.partial(swap_kernel, partner=partner), out_shape...  43.8 us
    pallas_call x4, Pallas kernels, cam_gather(): pl.pallas_call(cam_gather_kernel, out_shape=jax.ShapeDtypeStruct((4,) + b...  39 us
    all_to_all x1, waiting for transfers between devices, a2a_gather(): got = lax.all_to_all(tiled, axis_name, 0, 0, tiled=False)  19.1 us
    gather x4, local copies, waits for them, and re-layouts, local(): tile_rows = jnp.take(panel, tile_cam, axis=0)  11.5 us
  transfers between devices with their start and end apart: 1, of which 1 were waited for; matrix products, arithmetic and copies ran while one was open for 0% of the time, Pallas kernels for 0%

profile of v2, /device:TPU:0, one launch (start us, length us, event | category | flops | bytes accessed | tf_op | source)
XLA Modules:
  0.0 445.0 jit_solution(3666528267180226277)
XLA Ops:
  4.0 8.8 %all-to-all-start = ((bf16[32,1,32,576]{3,2,1,0:T(8,128)(2,1)}), bf16[32,1,32,576]{3,2,1,0:T(8,128)(2,1)S(1)}, u32[]{:S(2)}, u32[]{:S(2)}) async-start(bf16[32,1,32,576]{3,2,1,0:T(8,128)(2,1)} %broadcast_in_dim.26), calls=%async_computation | async-start | bytes 2621440 | tf_op jit(solution)/shard_map/all_to_all | solution.py:92
  12.9 19.1 %all-to-all-done = bf16[32,1,32,576]{3,2,1,0:T(8,128)(2,1)S(1)} async-done(((bf16[32,1,32,576]{3,2,1,0:T(8,128)(2,1)}), bf16[32,1,32,576]{3,2,1,0:T(8,128)(2,1)S(1)}, u32[]{:S(2)}, u32[]{:S(2)}) %all-to-all-start) | async-done | bytes 1179680 | tf_op jit(solution)/shard_map/all_to_all | solution.py:92
  32.0 2.9 gather_fusion
  34.9 11.7 %subtract_convert_fusion.7 = (bf16[80,32,192]{2,1,0:T(8,128)(2,1)S(1)}, bf16[80,32,192]{2,1,0:T(8,128)(2,1)S(1)}) fusion(bf16[80,576,192]{1,2,0:T(8,128)(2,1)} %param.12, bf16[80,32,576]{2,1,0:T(8,128)(2,1)} %gather_fusion, pred[80]{0:T(512)(128)(4,1)S(1)} %compare_and_fusion.1), kind=kOutput, calls=%fused_computation.47 | convolution fusion | flops 569671680 | bytes 22610000 | tf_op jit(solution)/shard_map/tpc,tcl->tpl/dot_general | solution.py:229
  54.4 9.1 %shard_map.65 = bf16[12,32,192]{2,1,0:T(8,128)(2,1)} custom-call(bf16[12,32,192]{2,1,0:T(8,128)(2,1)} %fusion.102.x_ref), custom_call_target="tpu_custom_call" | custom-call | tf_op jit(solution)/shard_map/pallas_call | solution.py:131
  63.5 2.4 convolution_convert_fusion.3.x_ref
  65.9 10.6 %shard_map.66 = bf16[4,12,32,192]{3,2,1,0:T(8,128)(2,1)} custom-call(bf16[12,32,192]{2,1,0:T(8,128)(2,1)} %convolution_convert_fusion.3.x_ref), custom_call_target="tpu_custom_call" | custom-call | tf_op jit(solution)/shard_map/pallas_call | solution.py:197
  78.3 11.3 %subtract_convert_fusion.3 = (bf16[80,32,576]{2,1,0:T(8,128)(2,1)S(1)}, bf16[80,32,576]{2,1,0:T(8,128)(2,1)S(1)}) fusion(bf16[80,576,192]{1,2,0:T(8,128)(2,1)} %param.12, bf16[80,32,192]{2,1,0:T(8,128)(2,1)S(1)} %gather_fusion.1, pred[80]{0:T(512)(128)(4,1)S(1)} %compare_and_fusion), kind=kOutput, calls=%fused_computation.11 | convolution fusion | flops 572620800 | bytes 24576080 | tf_op jit(solution)/shard_map/tpl,tcl->tpc/dot_general | solution.py:242
  93.1 25.7 %all_to_all.40 = bf16[32,1,32,576]{3,2,1,0:T(8,128)(2,1)S(1)} all-to-all(bf16[32,1,32,576]{3,2,1,0:T(8,128)(2,1)S(1)} %copy.58), channel_id=1, replica_groups=mesh['cam'=4,'lmk'=32] {'lmk'}, dimensions={0} | all-to-all | bytes 2359296 | tf_op jit(solution)/shard_map/all_to_all | solution.py:102
  119.4 23.8 %all_to_all.41 = bf16[32,1,32,576]{3,2,1,0:T(8,128)(2,1)S(1)} all-to-all(bf16[32,1,32,576]{3,2,1,0:T(8,128)(2,1)S(1)} %broadcast_in_dim.27), channel_id=1, replica_groups=mesh['cam'=4,'lmk'=32] {'lmk'}, dimensions={0} | all-to-all | bytes 2359296 | tf_op jit(solution)/shard_map/all_to_all | solution.py:92
  143.2 2.9 gather_fusion.2
  146.0 11.5 %subtract_convert_fusion.6 = (bf16[80,32,192]{2,1,0:T(8,128)(2,1)S(1)}, bf16[80,32,192]{2,1,0:T(8,128)(2,1)S(1)}) fusion(bf16[80,576,192]{1,2,0:T(8,128)(2,1)} %param.12, bf16[80,32,576]{2,1,0:T(8,128)(2,1)} %gather_fusion.2, pred[80]{0:T(512)(128)(4,1)S(1)} %compare_and_fusion.1), kind=kOutput, calls=%fused_computation.45 | convolution fusion | flops 569671680 | bytes 22610000 | tf_op jit(solution)/shard_map/tpc,tcl->tpl/dot_general | solution.py:229
  165.4 8.8 %shard_map.68 = bf16[12,32,192]{2,1,0:T(8,128)(2,1)} custom-call(bf16[12,32,192]{2,1,0:T(8,128)(2,1)} %fusion.103.x_ref), custom_call_target="tpu_custom_call" | custom-call | tf_op jit(solution)/shard_map/pallas_call | solution.py:131
  174.2 2.4 convolution_convert_fusion.2.x_ref
  176.5 9.5 %shard_map.69 = bf16[4,12,32,192]{3,2,1,0:T(8,128)(2,1)} custom-call(bf16[12,32,192]{2,1,0:T(8,128)(2,1)} %convolution_convert_fusion.2.x_ref), custom_call_target="tpu_custom_call" | custom-call | tf_op jit(solution)/shard_map/pallas_call | solution.py:197
  187.8 11.3 %subtract_convert_fusion.2 = (bf16[80,32,576]{2,1,0:T(8,128)(2,1)S(1)}, bf16[80,32,576]{2,1,0:T(8,128)(2,1)S(1)}) fusion(bf16[80,576,192]{1,2,0:T(8,128)(2,1)} %param.12, bf16[80,32,192]{2,1,0:T(8,128)(2,1)S(1)} %gather_fusion.3, pred[80]{0:T(512)(128)(4,1)S(1)} %compare_and_fusion), kind=kOutput, calls=%fused_computation.10 | convolution fusion | flops 572620800 | bytes 24576080 | tf_op jit(solution)/shard_map/tpl,tcl->tpc/dot_general | solution.py:242
  202.6 24.6 %all_to_all.42 = bf16[32,1,32,576]{3,2,1,0:T(8,128)(2,1)S(1)} all-to-all(bf16[32,1,32,576]{3,2,1,0:T(8,128)(2,1)S(1)} %copy.66), channel_id=1, replica_groups=mesh['cam'=4,'lmk'=32] {'lmk'}, dimensions={0} | all-to-all | bytes 2359296 | tf_op jit(solution)/shard_map/all_to_all | solution.py:102
  227.8 23.6 %all_to_all.43 = bf16[32,1,32,576]{3,2,1,0:T(8,128)(2,1)S(1)} all-to-all(bf16[32,1,32,576]{3,2,1,0:T(8,128)(2,1)S(1)} %broadcast_in_dim.28), channel_id=1, replica_groups=mesh['cam'=4,'lmk'=32] {'lmk'}, dimensions={0} | all-to-all | bytes 2359296 | tf_op jit(solution)/shard_map/all_to_all | solution.py:92
  251.3 2.9 gather_fusion.4
  254.2 11.5 %subtract_convert_fusion.5 = (bf16[80,32,192]{2,1,0:T(8,128)(2,1)S(1)}, bf16[80,32,192]{2,1,0:T(8,128)(2,1)S(1)}) fusion(bf16[80,576,192]{1,2,0:T(8,128)(2,1)} %param.12, bf16[80,32,576]{2,1,0:T(8,128)(2,1)} %gather_fusion.4, pred[80]{0:T(512)(128)(4,1)S(1)} %compare_and_fusion.1), kind=kOutput, calls=%fused_computation.43 | convolution fusion | flops 569671680 | bytes 22610000 | tf_op jit(solution)/shard_map/tpc,tcl->tpl/dot_general | solution.py:229
  273.5 8.8 %shard_map.71 = bf16[12,32,192]{2,1,0:T(8,128)(2,1)} custom-call(bf16[12,32,192]{2,1,0:T(8,128)(2,1)} %fusion.104.x_ref), custom_call_target="tpu_custom_call" | custom-call | tf_op jit(solution)/shard_map/pallas_call | solution.py:131
  282.3 2.4 convolution_convert_fusion.1.x_ref
  284.7 9.5 %shard_map.72 = bf16[4,12,32,192]{3,2,1,0:T(8,128)(2,1)} custom-call(bf16[12,32,192]{2,1,0:T(8,128)(2,1)} %convolution_convert_fusion.1.x_ref), custom_call_target="tpu_custom_call" | custom-call | tf_op jit(solution)/shard_map/pallas_call | solution.py:197
  296.0 11.3 %subtract_convert_fusion.1 = (bf16[80,32,576]{2,1,0:T(8,128)(2,1)S(1)}, bf16[80,32,576]{2,1,0:T(8,128)(2,1)S(1)}) fusion(bf16[80,576,192]{1,2,0:T(8,128)(2,1)} %param.12, bf16[80,32,192]{2,1,0:T(8,128)(2,1)S(1)} %gather_fusion.5, pred[80]{0:T(512)(128)(4,1)S(1)} %compare_and_fusion), kind=kOutput, calls=%fused_computation.9 | convolution fusion | flops 572620800 | bytes 24576080 | tf_op jit(solution)/shard_map/tpl,tcl->tpc/dot_general | solution.py:242
  310.8 24.5 %all_to_all.44 = bf16[32,1,32,576]{3,2,1,0:T(8,128)(2,1)S(1)} all-to-all(bf16[32,1,32,576]{3,2,1,0:T(8,128)(2,1)S(1)} %copy.74), channel_id=1, replica_groups=mesh['cam'=4,'lmk'=32] {'lmk'}, dimensions={0} | all-to-all | bytes 2359296 | tf_op jit(solution)/shard_map/all_to_all | solution.py:102
  335.9 23.6 %all_to_all.45 = bf16[32,1,32,576]{3,2,1,0:T(8,128)(2,1)S(1)} all-to-all(bf16[32,1,32,576]{3,2,1,0:T(8,128)(2,1)S(1)} %broadcast_in_dim.29), channel_id=1, replica_groups=mesh['cam'=4,'lmk'=32] {'lmk'}, dimensions={0} | all-to-all | bytes 2359296 | tf_op jit(solution)/shard_map/all_to_all | solution.py:92
  359.5 2.9 gather_fusion.6
  362.4 11.5 %subtract_convert_fusion.4 = (bf16[80,32,192]{2,1,0:T(8,128)(2,1)S(1)}, bf16[80,32,192]{2,1,0:T(8,128)(2,1)S(1)}) fusion(bf16[80,576,192]{1,2,0:T(8,128)(2,1)} %param.12, bf16[80,32,576]{2,1,0:T(8,128)(2,1)} %gather_fusion.6, pred[80]{0:T(512)(128)(4,1)S(1)} %compare_and_fusion.1), kind=kOutput, calls=%fused_computation.41 | convolution fusion | flops 569671680 | bytes 22610000 | tf_op jit(solution)/shard_map/tpc,tcl->tpl/dot_general | solution.py:229
  381.7 8.8 %shard_map.74 = bf16[12,32,192]{2,1,0:T(8,128)(2,1)} custom-call(bf16[12,32,192]{2,1,0:T(8,128)(2,1)} %fusion.105.x_ref), custom_call_target="tpu_custom_call" | custom-call | tf_op jit(solution)/shard_map/pallas_call | solution.py:131
  392.9 9.5 %shard_map.75 = bf16[4,12,32,192]{3,2,1,0:T(8,128)(2,1)} custom-call(bf16[12,32,192]{2,1,0:T(8,128)(2,1)} %convolution_convert_fusion.x_ref), custom_call_target="tpu_custom_call" | custom-call | tf_op jit(solution)/shard_map/pallas_call | solution.py:197
  404.2 11.3 %subtract_convert_fusion = (bf16[80,32,576]{2,1,0:T(8,128)(2,1)S(1)}, bf16[80,32,576]{2,1,0:T(8,128)(2,1)S(1)}) fusion(bf16[80,576,192]{1,2,0:T(8,128)(2,1)} %param.12, bf16[80,32,192]{2,1,0:T(8,128)(2,1)S(1)} %gather_fusion.7, pred[80]{0:T(512)(128)(4,1)S(1)} %compare_and_fusion), kind=kOutput, calls=%fused_computation.8 | convolution fusion | flops 572620800 | bytes 24576080 | tf_op jit(solution)/shard_map/tpl,tcl->tpc/dot_general | solution.py:242
  419.0 24.7 %all_to_all.46 = bf16[32,1,32,576]{3,2,1,0:T(8,128)(2,1)S(1)} all-to-all(bf16[32,1,32,576]{3,2,1,0:T(8,128)(2,1)S(1)} %copy.82), channel_id=1, replica_groups=mesh['cam'=4,'lmk'=32] {'lmk'}, dimensions={0} | all-to-all | bytes 2359296 | tf_op jit(solution)/shard_map/all_to_all | solution.py:102
  (72 shorter events, 61.6 us)
Async XLA Ops:
  0.0 1.1 copy-start
  0.0 12.8 %copy-start.2 = (s32[80]{0:T(128)S(1)}, s32[80]{0:T(128)}, u32[]{:S(2)}) copy-start(s32[80]{0:T(128)} %param.15) | copy-start | bytes 964
  0.0 12.8 %copy-start.3 = (s32[80]{0:T(128)S(1)}, s32[80]{0:T(128)}, u32[]{:S(2)}) copy-start(s32[80]{0:T(128)} %param.14) | copy-start | bytes 964
  4.0 28.0 %all-to-all-start = ((bf16[32,1,32,576]{3,2,1,0:T(8,128)(2,1)}), bf16[32,1,32,576]{3,2,1,0:T(8,128)(2,1)S(1)}, u32[]{:S(2)}, u32[]{:S(2)}) async-start(bf16[32,1,32,576]{3,2,1,0:T(8,128)(2,1)} %broadcast_in_dim.26), calls=%async_computation | async-start | bytes 2621440 | tf_op jit(solution)/shard_map/all_to_all | solution.py:92
  419.0 24.9 %copy-start.1 = (f32[32,576]{1,0:T(8,128)S(1)}, f32[32,576]{1,0:T(8,128)}, u32[]{:S(2)}) copy-start(f32[32,576]{1,0:T(8,128)} %get-tuple-element.24) | copy-start | bytes 221188

commit v3 on v2

--- a/solution.py
+++ b/solution.py
@@ -142,16 +142,66 @@
     return jnp.where(flag == 0, a, b)
 
 
+def cam_reduce_kernel(x_ref, o_ref, send_one, recv_one, chip_ref, send_two, recv_two, send_sem, recv_sem):
+    cam = lax.axis_index("cam")
+    lmk = lax.axis_index("lmk")
+    core, high = cam % 2, cam // 2
+    core_peer, high_peer = cam ^ 1, cam ^ 2
+    send_one[...] = x_ref[1 - core].astype(send_one.dtype)
+    barrier = pltpu.get_barrier_semaphore()
+    for peer in (core_peer, high_peer):
+        pl.semaphore_signal(barrier, inc=1, device_id=(peer, lmk), device_id_type=MESH)
+    pl.semaphore_wait(barrier, 2)
+    first = pltpu.make_async_remote_copy(
+        src_ref=send_one,
+        dst_ref=recv_one,
+        send_sem=send_sem.at[0],
+        recv_sem=recv_sem.at[0],
+        device_id=(core_peer, lmk),
+        device_id_type=MESH,
+    )
+    first.start()
+    first.wait_send()
+    first.wait_recv()
+    chip_ref[...] = x_ref[core] + recv_one[...].astype(jnp.float32)
+    send_two[...] = chip_ref[1 - high].astype(send_two.dtype)
+    second = pltpu.make_async_remote_copy(
+        src_ref=send_two,
+        dst_ref=recv_two,
+        send_sem=send_sem.at[1],
+        recv_sem=recv_sem.at[1],
+        device_id=(high_peer, lmk),
+        device_id_type=MESH,
+    )
+    second.start()
+    second.wait_send()
+    second.wait_recv()
+    o_ref[...] = chip_ref[high] + recv_two[...].astype(jnp.float32)
+
+
 def cam_reduce(partial_value):
-    cam = lax.axis_index("cam")
-    core, high = cam % 2, cam // 2
-    chunks = partial_value.reshape((2, 2, partial_value.shape[0] // 4) + partial_value.shape[1:])
-    mine = pick(core, chunks[:, 0], chunks[:, 1])
-    theirs = pick(core, chunks[:, 1], chunks[:, 0])
-    chip = mine + swap(theirs.astype(jnp.bfloat16), 1).astype(jnp.float32)
-    keep = pick(high, chip[0], chip[1])
-    send = pick(high, chip[1], chip[0])
-    return keep + swap(send.astype(jnp.bfloat16), 2).astype(jnp.float32)
+    chunk = partial_value.shape[0] // 4
+    rest = partial_value.shape[1:]
+    chunks = partial_value.reshape((2, 2, chunk) + rest).swapaxes(0, 1)
+    key = ("cam_reduce", chunks.shape)
+    if key not in COLLECTIVE_IDS:
+        COLLECTIVE_IDS[key] = len(COLLECTIVE_IDS)
+    return pl.pallas_call(
+        cam_reduce_kernel,
+        out_shape=jax.ShapeDtypeStruct((chunk,) + rest, jnp.float32),
+        in_specs=[pl.BlockSpec(memory_space=pltpu.VMEM)],
+        out_specs=pl.BlockSpec(memory_space=pltpu.VMEM),
+        scratch_shapes=[
+            pltpu.VMEM((2, chunk) + rest, jnp.bfloat16),
+            pltpu.VMEM((2, chunk) + rest, jnp.bfloat16),
+            pltpu.VMEM((2, chunk) + rest, jnp.float32),
+            pltpu.VMEM((chunk,) + rest, jnp.bfloat16),
+            pltpu.VMEM((chunk,) + rest, jnp.bfloat16),
+            pltpu.SemaphoreType.DMA((2,)),
+            pltpu.SemaphoreType.DMA((2,)),
+        ],
+        compiler_params=pltpu.CompilerParams(collective_id=COLLECTIVE_IDS[key], has_side_effects=True),
+    )(chunks)
 
 
 def cam_gather_kernel(x_ref, o_ref, send_sem, recv_sem, local_sem):

time: 449 us -> 452 us (level)
  other arithmetic: 11.9 us -> 0.84 us
  Pallas kernels: 82.8 us -> 91.8 us
  local copies, waits for them, and re-layouts: 26.7 us -> 31.8 us
    pallas_call x8 -> x4, Pallas kernels: 43.8 us -> 51.1 us  [cam_reduce(): pl.pallas_call(cam_reduce_kernel, out_shape=jax.ShapeDtypeStruct((chunk,)...]
    convert_element_type x8 -> x0, other arithmetic: 6.23 us -> none  [the longest x4 3.32 us: cam_reduce(): chip = mine + swap(theirs.astype(jnp.bfloat16), 1).astype(jnp.float32)]
    reshape x0 -> x4, local copies, waits for them, and re-layouts: none -> 5.06 us  [cam_reduce(): chunks = partial_value.reshape((2, 2, chunk) + rest).swapaxes(0, 1)]
    add x4 -> x0, other arithmetic: 4.82 us -> none  [cam_reduce(): chip = mine + swap(theirs.astype(jnp.bfloat16), 1).astype(jnp.float32)]
where the time goes in v3:
time: 452 us; the launch traced here: 448 us
  blocking collectives  170 us (38%)
  matrix products  125 us (28%)
  Pallas kernels  91.8 us (20%)
  local copies, waits for them, and re-layouts  31.8 us (7%)
  waiting for transfers between devices  19.1 us (4%)
  starting transfers between devices  8.78 us (2%)
    all_to_all x4, blocking collectives, a2a_reduce_scatter(): lax.all_to_all(chunks.astype(jnp.bfloat16), axis_name, 0, 0, tiled=False)  99.5 us
    all_to_all x3, blocking collectives, a2a_gather(): got = lax.all_to_all(tiled, axis_name, 0, 0, tiled=False)  71 us
    pallas_call x4, Pallas kernels, cam_reduce(): pl.pallas_call(cam_reduce_kernel, out_shape=jax.ShapeDtypeStruct((chunk,)...  51.1 us
    dot_general x4, matrix products, local(): jnp.einsum('tpc,tcl->tpl', tile_rows, couplings, preferred_element_type=j...  46.3 us
    dot_general x4, matrix products, local(): jnp.einsum('tpl,tcl->tpc', picked, couplings, preferred_element_type=jnp....  45 us
    pallas_call x4, Pallas kernels, cam_gather(): pl.pallas_call(cam_gather_kernel, out_shape=jax.ShapeDtypeStruct((4,) + b...  40.7 us
    all_to_all x1, waiting for transfers between devices, a2a_gather(): got = lax.all_to_all(tiled, axis_name, 0, 0, tiled=False)  19.1 us
    gather x4, local copies, waits for them, and re-layouts, local(): tile_rows = jnp.take(panel, tile_cam, axis=0)  11.5 us
  transfers between devices with their start and end apart: 1, of which 1 were waited for; matrix products, arithmetic and copies ran while one was open for 0% of the time, Pallas kernels for 0%

profile of v3, /device:TPU:0, one launch (start us, length us, event | category | flops | bytes accessed | tf_op | source)
XLA Modules:
  0.0 448.1 jit_solution(17717737264143892876)
XLA Ops:
  4.0 8.8 %all-to-all-start = ((bf16[32,1,32,576]{3,2,1,0:T(8,128)(2,1)}), bf16[32,1,32,576]{3,2,1,0:T(8,128)(2,1)S(1)}, u32[]{:S(2)}, u32[]{:S(2)}) async-start(bf16[32,1,32,576]{3,2,1,0:T(8,128)(2,1)} %broadcast_in_dim.26), calls=%async_computation | async-start | bytes 2621440 | tf_op jit(solution)/shard_map/all_to_all | solution.py:92
  12.8 19.1 %all-to-all-done = bf16[32,1,32,576]{3,2,1,0:T(8,128)(2,1)S(1)} async-done(((bf16[32,1,32,576]{3,2,1,0:T(8,128)(2,1)}), bf16[32,1,32,576]{3,2,1,0:T(8,128)(2,1)S(1)}, u32[]{:S(2)}, u32[]{:S(2)}) %all-to-all-start) | async-done | bytes 1179680 | tf_op jit(solution)/shard_map/all_to_all | solution.py:92
  32.0 2.9 gather_fusion
  34.9 11.7 %subtract_convert_fusion.7 = (bf16[80,32,192]{2,1,0:T(8,128)(2,1)S(1)}, bf16[80,32,192]{2,1,0:T(8,128)(2,1)S(1)}) fusion(bf16[80,576,192]{1,2,0:T(8,128)(2,1)} %param.12, bf16[80,32,576]{2,1,0:T(8,128)(2,1)} %gather_fusion, pred[80]{0:T(512)(128)(4,1)S(1)} %compare_and_fusion.1), kind=kOutput, calls=%fused_computation.47 | convolution fusion | flops 569671680 | bytes 22610000 | tf_op jit(solution)/shard_map/tpc,tcl->tpl/dot_general | solution.py:279
  50.8 12.9 %shard_map.64 = f32[12,32,192]{2,1,0:T(8,128)} custom-call(f32[2,2,12,32,192]{4,3,2,1,0:T(8,128)} %bitcast.98), custom_call_target="tpu_custom_call" | custom-call | tf_op jit(solution)/shard_map/pallas_call | solution.py:189
  63.7 2.4 convolution_convert_fusion.3.x_ref
  66.1 10.8 %shard_map.65 = bf16[4,12,32,192]{3,2,1,0:T(8,128)(2,1)} custom-call(bf16[12,32,192]{2,1,0:T(8,128)(2,1)} %convolution_convert_fusion.3.x_ref), custom_call_target="tpu_custom_call" | custom-call | tf_op jit(solution)/shard_map/pallas_call | solution.py:247
  78.7 11.3 %subtract_convert_fusion.3 = (bf16[80,32,576]{2,1,0:T(8,128)(2,1)S(1)}, bf16[80,32,576]{2,1,0:T(8,128)(2,1)S(1)}) fusion(bf16[80,576,192]{1,2,0:T(8,128)(2,1)} %param.12, bf16[80,32,192]{2,1,0:T(8,128)(2,1)S(1)} %gather_fusion.1, pred[80]{0:T(512)(128)(4,1)S(1)} %compare_and_fusion), kind=kOutput, calls=%fused_computation.11 | convolution fusion | flops 572620800 | bytes 24576080 | tf_op jit(solution)/shard_map/tpl,tcl->tpc/dot_general | solution.py:292
  93.5 25.7 %all_to_all.40 = bf16[32,1,32,576]{3,2,1,0:T(8,128)(2,1)S(1)} all-to-all(bf16[32,1,32,576]{3,2,1,0:T(8,128)(2,1)S(1)} %copy.53), channel_id=1, replica_groups=mesh['cam'=4,'lmk'=32] {'lmk'}, dimensions={0} | all-to-all | bytes 2359296 | tf_op jit(solution)/shard_map/all_to_all | solution.py:102
  119.8 23.8 %all_to_all.41 = bf16[32,1,32,576]{3,2,1,0:T(8,128)(2,1)S(1)} all-to-all(bf16[32,1,32,576]{3,2,1,0:T(8,128)(2,1)S(1)} %broadcast_in_dim.27), channel_id=1, replica_groups=mesh['cam'=4,'lmk'=32] {'lmk'}, dimensions={0} | all-to-all | bytes 2359296 | tf_op jit(solution)/shard_map/all_to_all | solution.py:92
  143.6 2.9 gather_fusion.2
  146.4 11.5 %subtract_convert_fusion.6 = (bf16[80,32,192]{2,1,0:T(8,128)(2,1)S(1)}, bf16[80,32,192]{2,1,0:T(8,128)(2,1)S(1)}) fusion(bf16[80,576,192]{1,2,0:T(8,128)(2,1)} %param.12, bf16[80,32,576]{2,1,0:T(8,128)(2,1)} %gather_fusion.2, pred[80]{0:T(512)(128)(4,1)S(1)} %compare_and_fusion.1), kind=kOutput, calls=%fused_computation.45 | convolution fusion | flops 569671680 | bytes 22610000 | tf_op jit(solution)/shard_map/tpc,tcl->tpl/dot_general | solution.py:279
  162.2 12.7 %shard_map.66 = f32[12,32,192]{2,1,0:T(8,128)} custom-call(f32[2,2,12,32,192]{4,3,2,1,0:T(8,128)} %bitcast.99), custom_call_target="tpu_custom_call" | custom-call | tf_op jit(solution)/shard_map/pallas_call | solution.py:189
  174.9 2.4 convolution_convert_fusion.2.x_ref
  177.3 10.0 %shard_map.67 = bf16[4,12,32,192]{3,2,1,0:T(8,128)(2,1)} custom-call(bf16[12,32,192]{2,1,0:T(8,128)(2,1)} %convolution_convert_fusion.2.x_ref), custom_call_target="tpu_custom_call" | custom-call | tf_op jit(solution)/shard_map/pallas_call | solution.py:247
  189.1 11.3 %subtract_convert_fusion.2 = (bf16[80,32,576]{2,1,0:T(8,128)(2,1)S(1)}, bf16[80,32,576]{2,1,0:T(8,128)(2,1)S(1)}) fusion(bf16[80,576,192]{1,2,0:T(8,128)(2,1)} %param.12, bf16[80,32,192]{2,1,0:T(8,128)(2,1)S(1)} %gather_fusion.3, pred[80]{0:T(512)(128)(4,1)S(1)} %compare_and_fusion), kind=kOutput, calls=%fused_computation.10 | convolution fusion | flops 572620800 | bytes 24576080 | tf_op jit(solution)/shard_map/tpl,tcl->tpc/dot_general | solution.py:292
  203.9 24.6 %all_to_all.42 = bf16[32,1,32,576]{3,2,1,0:T(8,128)(2,1)S(1)} all-to-all(bf16[32,1,32,576]{3,2,1,0:T(8,128)(2,1)S(1)} %copy.60), channel_id=1, replica_groups=mesh['cam'=4,'lmk'=32] {'lmk'}, dimensions={0} | all-to-all | bytes 2359296 | tf_op jit(solution)/shard_map/all_to_all | solution.py:102
  229.1 23.6 %all_to_all.43 = bf16[32,1,32,576]{3,2,1,0:T(8,128)(2,1)S(1)} all-to-all(bf16[32,1,32,576]{3,2,1,0:T(8,128)(2,1)S(1)} %broadcast_in_dim.28), channel_id=1, replica_groups=mesh['cam'=4,'lmk'=32] {'lmk'}, dimensions={0} | all-to-all | bytes 2359296 | tf_op jit(solution)/shard_map/all_to_all | solution.py:92
  252.6 2.9 gather_fusion.4
  255.5 11.5 %subtract_convert_fusion.5 = (bf16[80,32,192]{2,1,0:T(8,128)(2,1)S(1)}, bf16[80,32,192]{2,1,0:T(8,128)(2,1)S(1)}) fusion(bf16[80,576,192]{1,2,0:T(8,128)(2,1)} %param.12, bf16[80,32,576]{2,1,0:T(8,128)(2,1)} %gather_fusion.4, pred[80]{0:T(512)(128)(4,1)S(1)} %compare_and_fusion.1), kind=kOutput, calls=%fused_computation.43 | convolution fusion | flops 569671680 | bytes 22610000 | tf_op jit(solution)/shard_map/tpc,tcl->tpl/dot_general | solution.py:279
  271.2 12.7 %shard_map.68 = f32[12,32,192]{2,1,0:T(8,128)} custom-call(f32[2,2,12,32,192]{4,3,2,1,0:T(8,128)} %bitcast.100), custom_call_target="tpu_custom_call" | custom-call | tf_op jit(solution)/shard_map/pallas_call | solution.py:189
  284.0 2.4 convolution_convert_fusion.1.x_ref
  286.4 10.0 %shard_map.69 = bf16[4,12,32,192]{3,2,1,0:T(8,128)(2,1)} custom-call(bf16[12,32,192]{2,1,0:T(8,128)(2,1)} %convolution_convert_fusion.1.x_ref), custom_call_target="tpu_custom_call" | custom-call | tf_op jit(solution)/shard_map/pallas_call | solution.py:247
  298.2 11.3 %subtract_convert_fusion.1 = (bf16[80,32,576]{2,1,0:T(8,128)(2,1)S(1)}, bf16[80,32,576]{2,1,0:T(8,128)(2,1)S(1)}) fusion(bf16[80,576,192]{1,2,0:T(8,128)(2,1)} %param.12, bf16[80,32,192]{2,1,0:T(8,128)(2,1)S(1)} %gather_fusion.5, pred[80]{0:T(512)(128)(4,1)S(1)} %compare_and_fusion), kind=kOutput, calls=%fused_computation.9 | convolution fusion | flops 572620800 | bytes 24576080 | tf_op jit(solution)/shard_map/tpl,tcl->tpc/dot_general | solution.py:292
  313.0 24.6 %all_to_all.44 = bf16[32,1,32,576]{3,2,1,0:T(8,128)(2,1)S(1)} all-to-all(bf16[32,1,32,576]{3,2,1,0:T(8,128)(2,1)S(1)} %copy.67), channel_id=1, replica_groups=mesh['cam'=4,'lmk'=32] {'lmk'}, dimensions={0} | all-to-all | bytes 2359296 | tf_op jit(solution)/shard_map/all_to_all | solution.py:102
  338.1 23.6 %all_to_all.45 = bf16[32,1,32,576]{3,2,1,0:T(8,128)(2,1)S(1)} all-to-all(bf16[32,1,32,576]{3,2,1,0:T(8,128)(2,1)S(1)} %broadcast_in_dim.29), channel_id=1, replica_groups=mesh['cam'=4,'lmk'=32] {'lmk'}, dimensions={0} | all-to-all | bytes 2359296 | tf_op jit(solution)/shard_map/all_to_all | solution.py:92
  361.7 2.9 gather_fusion.6
  364.6 11.5 %subtract_convert_fusion.4 = (bf16[80,32,192]{2,1,0:T(8,128)(2,1)S(1)}, bf16[80,32,192]{2,1,0:T(8,128)(2,1)S(1)}) fusion(bf16[80,576,192]{1,2,0:T(8,128)(2,1)} %param.12, bf16[80,32,576]{2,1,0:T(8,128)(2,1)} %gather_fusion.6, pred[80]{0:T(512)(128)(4,1)S(1)} %compare_and_fusion.1), kind=kOutput, calls=%fused_computation.41 | convolution fusion | flops 569671680 | bytes 22610000 | tf_op jit(solution)/shard_map/tpc,tcl->tpl/dot_general | solution.py:279
  380.3 12.7 %shard_map.70 = f32[12,32,192]{2,1,0:T(8,128)} custom-call(f32[2,2,12,32,192]{4,3,2,1,0:T(8,128)} %bitcast.101), custom_call_target="tpu_custom_call" | custom-call | tf_op jit(solution)/shard_map/pallas_call | solution.py:189
  395.5 10.0 %shard_map.71 = bf16[4,12,32,192]{3,2,1,0:T(8,128)(2,1)} custom-call(bf16[12,32,192]{2,1,0:T(8,128)(2,1)} %convolution_convert_fusion.x_ref), custom_call_target="tpu_custom_call" | custom-call | tf_op jit(solution)/shard_map/pallas_call | solution.py:247
  407.3 11.3 %subtract_convert_fusion = (bf16[80,32,576]{2,1,0:T(8,128)(2,1)S(1)}, bf16[80,32,576]{2,1,0:T(8,128)(2,1)S(1)}) fusion(bf16[80,576,192]{1,2,0:T(8,128)(2,1)} %param.12, bf16[80,32,192]{2,1,0:T(8,128)(2,1)S(1)} %gather_fusion.7, pred[80]{0:T(512)(128)(4,1)S(1)} %compare_and_fusion), kind=kOutput, calls=%fused_computation.8 | convolution fusion | flops 572620800 | bytes 24576080 | tf_op jit(solution)/shard_map/tpl,tcl->tpc/dot_general | solution.py:292
  422.1 24.7 %all_to_all.46 = bf16[32,1,32,576]{3,2,1,0:T(8,128)(2,1)S(1)} all-to-all(bf16[32,1,32,576]{3,2,1,0:T(8,128)(2,1)S(1)} %copy.74), channel_id=1, replica_groups=mesh['cam'=4,'lmk'=32] {'lmk'}, dimensions={0} | all-to-all | bytes 2359296 | tf_op jit(solution)/shard_map/all_to_all | solution.py:102
  (60 shorter events, 47.3 us)
Async XLA Ops:
  0.0 1.1 copy-start
  0.0 12.8 %copy-start.2 = (s32[80]{0:T(128)S(1)}, s32[80]{0:T(128)}, u32[]{:S(2)}) copy-start(s32[80]{0:T(128)} %param.15) | copy-start | bytes 964
  0.0 12.8 %copy-start.3 = (s32[80]{0:T(128)S(1)}, s32[80]{0:T(128)}, u32[]{:S(2)}) copy-start(s32[80]{0:T(128)} %param.14) | copy-start | bytes 964
  4.0 28.0 %all-to-all-start = ((bf16[32,1,32,576]{3,2,1,0:T(8,128)(2,1)}), bf16[32,1,32,576]{3,2,1,0:T(8,128)(2,1)S(1)}, u32[]{:S(2)}, u32[]{:S(2)}) async-start(bf16[32,1,32,576]{3,2,1,0:T(8,128)(2,1)} %broadcast_in_dim.26), calls=%async_computation | async-start | bytes 2621440 | tf_op jit(solution)/shard_map/all_to_all | solution.py:92
  422.1 24.9 %copy-start.1 = (f32[32,576]{1,0:T(8,128)S(1)}, f32[32,576]{1,0:T(8,128)}, u32[]{:S(2)}) copy-start(f32[32,576]{1,0:T(8,128)} %get-tuple-element.24) | copy-start | bytes 221188
